TPU v7x, 256 devices: a whole 4x4x8 slice. The times are simulated.
256 devices in a mesh: coil: 32 (over z, y), slab: 8 (over x, core).
Axes of the slice: x: 4, y: 4, z: 8, core: 2. Of those that a mesh axis runs over, the one named last changes fastest.
Arguments:
- cotangent: float32 [32, 2, 256, 256], P('coil', None, 'slab'), may hold values from -60 to 60
- saved_solution: float32 [32, 2, 256, 256], P('coil', None, 'slab'), may hold values from -6 to 6
- coil_maps: bfloat16 [32, 32, 2, 256, 256], P('coil', None, None, 'slab'), may hold values from -1.5 to 1.5
- kspace: bfloat16 [32, 32, 2, 256, 256], P('coil', None, None, 'slab'), may hold values from -6 to 6
- mask_logit: float32 [32, 256], P(None, 'slab'), may hold values from -4.5 to 4.5
- reach: int32 [32, 256], P(None, 'slab'), may hold values from 0 to 256, as said below
Outputs:
- image_grad: float32 [32, 2, 256, 256], P('coil', None, 'slab')
- kspace_grad: bfloat16 [32, 32, 2, 256, 256], P('coil', None, None, 'slab')
- logit_grad: float32 [32, 256], P(None, 'slab')
Inputs may be any that keep to these rules, and one draw needn't show every extreme that they name: reach[z, y] is 0 (line not acquired) or between 128 and 256; line [0, 0] is always fully acquired and line [0, 128] never.
All inputs are finite; a program needn't handle non-finite values.
Results may differ from a plain program's by a relative error of at most 0.02.
Values may be sent and summed in bfloat16 or wider, within the bound.
A program may use at most 64 MiB of HBM per device.

v0:
```python
import math
import jax
import jax.numpy as jnp
from jax import lax
from jax.sharding import PartitionSpec as P

NX = 256
NY = 256
NZ = 32
ITERS = 2
DAMPING = 0.2


def dft_table(length, sign):
    index = jnp.arange(length, dtype=jnp.int32)
    phase = (index[:, None] * index[None, :] % length).astype(jnp.float32) * (
        2.0 * math.pi / length
    )
    factor = 1.0 / math.sqrt(length)
    cosine = jnp.cos(phase) * factor
    sine = sign * jnp.sin(phase) * factor
    table = jnp.stack(
        [jnp.stack([cosine, sine], axis=1), jnp.stack([-sine, cosine], axis=1)], axis=0
    )
    return table.astype(jnp.bfloat16)


def complex_product(factor, operand):
    factor_re, factor_im = (factor[:, 0], factor[:, 1])
    operand_re, operand_im = (operand[:, 0], operand[:, 1])
    return jnp.stack(
        [
            factor_re * operand_re - factor_im * operand_im,
            factor_re * operand_im + factor_im * operand_re,
        ],
        axis=1,
    )


def conjugate_product(factor, operand):
    factor_re, factor_im = (factor[:, 0], factor[:, 1])
    operand_re, operand_im = (operand[:, 0], operand[:, 1])
    return jnp.stack(
        [
            factor_re * operand_re + factor_im * operand_im,
            factor_re * operand_im - factor_im * operand_re,
        ],
        axis=1,
    )


def shards(cotangent, saved_solution, coil_maps, kspace, mask_logit, reach):
    y_fwd, y_inv = (dft_table(NY, -1.0), dft_table(NY, 1.0))
    z_fwd, z_inv = (dft_table(NZ, -1.0), dft_table(NZ, 1.0))
    x_fwd, x_inv = (dft_table(NX, -1.0), dft_table(NX, 1.0))
    maps = coil_maps[0]
    data = kspace[0].astype(jnp.float32)
    readout = jnp.arange(NX, dtype=jnp.int32)
    centred = (readout + NX // 2) % NX
    sampled = (centred[None, None, :] >= (NX - reach)[:, :, None]).astype(jnp.float32)
    gate = jax.nn.sigmoid(mask_logit)
    weight = sampled * gate[:, :, None]
    squared = (weight * weight)[:, None]

    def front(piece):
        product = complex_product(maps.astype(jnp.float32), piece.astype(jnp.float32)).astype(
            jnp.bfloat16
        )
        return jnp.einsum(
            "zixn,inok->zoxk", product, y_fwd, preferred_element_type=jnp.float32
        ).astype(jnp.bfloat16)

    def gathered_front(shard):
        return front(lax.all_gather(shard, "coil", axis=0, tiled=True))

    def to_kspace(rows):
        mixed = jnp.einsum(
            "nixk,inom->moxk", rows, z_fwd, preferred_element_type=jnp.float32
        ).astype(jnp.bfloat16)
        swapped = lax.all_to_all(mixed, "slab", split_axis=3, concat_axis=2, tiled=True)
        return jnp.einsum("zink,inoq->zokq", swapped, x_fwd, preferred_element_type=jnp.float32)

    direction = cotangent
    both = ("coil", "slab")
    saved_k = to_kspace(gathered_front(saved_solution.astype(jnp.bfloat16)))
    first_k = to_kspace(gathered_front(direction.astype(jnp.bfloat16)))
    first_w = weight[:, None] * first_k
    norm_now, first_energy = lax.psum(
        (jnp.sum(direction * direction), jnp.sum(first_w * first_w)), both
    )
    apply_spectrum = (squared * first_k).astype(jnp.bfloat16)
    to_mixed = jnp.einsum(
        "zikq,iqon->zonk", apply_spectrum, x_inv, preferred_element_type=jnp.float32
    ).astype(jnp.bfloat16)
    to_swapped = lax.all_to_all(to_mixed, "slab", split_axis=2, concat_axis=3, tiled=True)
    apply_image_rows = jnp.einsum(
        "mixk,imon->noxk", to_swapped, z_inv, preferred_element_type=jnp.float32
    ).astype(jnp.bfloat16)
    image = jnp.einsum(
        "zixk,ikon->zoxn", apply_image_rows, y_inv, preferred_element_type=jnp.float32
    )
    summed = lax.psum_scatter(
        conjugate_product(maps.astype(jnp.float32), image).astype(jnp.bfloat16),
        "coil",
        scatter_dimension=0,
        tiled=True,
    ).astype(jnp.float32)
    image = summed + DAMPING * direction
    alpha = norm_now / (first_energy + DAMPING * norm_now)
    residual = direction - alpha * image
    second_k = to_kspace(gathered_front(residual.astype(jnp.bfloat16)))
    second_w = weight[:, None] * second_k
    gain = gate * (1.0 - gate)
    target = data - 2.0 * weight[:, None] * saved_k

    def line_terms(spectrum):
        return gain * jnp.sum(sampled * jnp.sum(spectrum * target, axis=1), axis=2)

    norm_next, crossing, second_energy, mixed_energy = lax.psum(
        (
            jnp.sum(residual * residual),
            jnp.sum(residual * direction),
            jnp.sum(second_w * second_w),
            jnp.sum(second_w * first_w),
        ),
        both,
    )
    lines = lax.psum(jnp.stack([line_terms(first_k), line_terms(second_k)]), "coil")
    beta = norm_next / norm_now
    curvature = (
        second_energy
        + beta * (2.0 * mixed_energy + beta * first_energy)
        + DAMPING * (norm_next + beta * (2.0 * crossing + beta * norm_now))
    )
    later = norm_next / curvature
    early = alpha + later * beta
    image_grad = DAMPING * (early * direction + later * residual)
    kspace_grad = (early * first_w + later * second_w).astype(jnp.bfloat16)[None]
    logit_grad = early * lines[0] + later * lines[1]
    return (image_grad, kspace_grad, logit_grad)


def solution(mesh):
    placed = (
        P("coil", None, "slab", None),
        P("coil", None, "slab", None),
        P("coil", None, None, "slab", None),
        P("coil", None, None, "slab", None),
        P(None, "slab"),
        P(None, "slab"),
    )
    return jax.shard_map(
        shards,
        mesh=mesh,
        in_specs=placed,
        out_specs=(
            P("coil", None, "slab", None),
            P("coil", None, None, "slab", None),
            P(None, "slab"),
        ),
        check_vma=False,
    )
```

profile of v0, /device:TPU:2, one launch (start us, length us, event | category | flops | bytes accessed | tf_op | source)
XLA Modules:
  0.0 753.5 jit_solution(7913596652548034315)
XLA Ops:
  7.2 2.1 fusion.89
  14.3 1.8 bitcast_convert_fusion.8
  16.2 74.3 %all-gather.4.cloned.1.call-done = bf16[32,2,32,256]{3,2,1,0:T(8,128)(2,1)} async-done(((bf16[1,2,32,256]{3,2,1,0:T(8,128)(2,1)}), bf16[32,2,32,256]{3,2,1,0:T(8,128)(2,1)}) %all-gather.4.cloned.1.call-update) | async-done | bytes 1048592 | tf_op jit(solution)/shard_map/all_gather | solution.py:74
  90.6 1.8 copy_convert_fusion.2
  93.9 3.2 fusion.4
  97.1 7.2 copy.81
  104.3 7.8 %reshape.272 = bf16[8,2,32768]{2,1,0:T(2,128)(2,1)} reshape(bf16[256,2,32,32]{3,2,1,0:T(8,128)(2,1)} %bitcast.296) | data formatting | bytes 2097152
  112.2 5.5 all-to-all-start
  120.4 11.7 %all-to-all-done = bf16[8,2,32768]{2,1,0:T(2,128)(2,1)} async-done(((bf16[8,2,32768]{2,1,0:T(2,128)(2,1)}), bf16[8,2,32768]{2,1,0:T(2,128)(2,1)}, u32[]{:S(2)}, u32[]{:S(2)}) %all-to-all-start) | async-done | bytes 1048608 | tf_op jit(solution)/shard_map/all_to_all | solution.py:80
  132.1 7.0 reshape.273
  139.1 6.7 copy.82
  145.9 6.2 reshape.243
  152.0 4.4 fusion.2
  158.1 7.2 copy.85
  165.3 7.8 %reshape.274 = bf16[8,2,32768]{2,1,0:T(2,128)(2,1)} reshape(bf16[256,2,32,32]{3,2,1,0:T(8,128)(2,1)} %bitcast.297) | data formatting | bytes 2097152
  173.2 5.6 all-to-all-start.1
  178.9 3.2 copy_convert_fusion
  182.1 11.2 %all-to-all-done.1 = bf16[8,2,32768]{2,1,0:T(2,128)(2,1)} async-done(((bf16[8,2,32768]{2,1,0:T(2,128)(2,1)}), bf16[8,2,32768]{2,1,0:T(2,128)(2,1)}, u32[]{:S(2)}, u32[]{:S(2)}) %all-to-all-start.1) | async-done | bytes 1048608 | tf_op jit(solution)/shard_map/all_to_all | solution.py:95
  193.3 7.0 reshape.275
  200.4 6.9 copy.160
  207.2 6.2 all_to_all.59
  213.4 2.2 fusion.5
  217.2 1.9 subtract_convert_fusion
  221.5 73.8 %all-reduce.2 = (f32[]{:T(128)}, f32[]{:T(128)}) all-reduce(f32[]{:T(128)} %get-tuple-element.49, f32[]{:T(128)} %get-tuple-element.40), channel_id=1, replica_groups=mesh['coil'=32,'slab'=8] {'coil','slab'}, use_global_device_ids=true, to_apply=%region_1.2 | all-reduce | flops 2 | bytes 16 | tf_op jit(solution)/shard_map/psum | solution.py:88
  297.2 71.0 %all-reduce.5.cloned.1.call-done = bf16[32,2,32,256]{3,2,0,1:T(8,128)(2,1)} async-done(((bf16[32,2,32,256]{3,2,0,1:T(8,128)(2,1)}), bf16[32,2,32,256]{3,2,0,1:T(8,128)(2,1)}) %all-reduce.5.cloned.1.call-update) | async-done | bytes 1048592
  368.2 2.7 fusion.61
  370.9 3.3 fusion.7
  374.1 7.2 copy.103
  381.4 7.8 %reshape.278 = bf16[8,2,32768]{2,1,0:T(2,128)(2,1)} reshape(bf16[256,2,32,32]{3,2,1,0:T(8,128)(2,1)} %bitcast.298) | data formatting | bytes 2097152
  389.2 5.1 all-to-all-start.3
  394.3 50.5 %all-gather.6.cloned.1.call-done = bf16[32,2,32,256]{3,2,1,0:T(8,128)(2,1)} async-done(((bf16[1,2,32,256]{3,2,1,0:T(8,128)(2,1)}), bf16[32,2,32,256]{3,2,1,0:T(8,128)(2,1)}) %all-gather.6.cloned.1.call-update) | async-done | bytes 1048592 | tf_op jit(solution)/shard_map/all_gather | solution.py:74
  448.2 2.3 fusion.6
  450.5 6.5 copy.97
  457.0 7.8 %reshape.276 = bf16[8,2,32768]{2,1,0:T(2,128)(2,1)} reshape(bf16[256,2,32,32]{3,2,1,0:T(8,128)(2,1)} %bitcast.299) | data formatting | bytes 2097152
  464.8 4.8 all-to-all-start.2
  469.6 7.0 reshape.279
  476.6 6.7 copy.104
  483.3 5.4 reshape.264
  488.7 3.4 fusion
  492.1 7.0 reshape.277
  499.1 6.7 copy.98
  505.8 6.3 reshape.258
  512.1 6.2 multiply_reduce_fusion
  518.3 74.5 %all-reduce.1 = (f32[]{:T(128)}, f32[]{:T(128)}, f32[]{:T(128)}, f32[]{:T(128)}) all-reduce(f32[]{:T(128)} %get-tuple-element.20, f32[]{:T(128)} %get-tuple-element.16, f32[]{:T(128)} %get-tuple-element.15, f32[]{:T(128)} %get-tuple-element.19), channel_id=1, replica_groups=mesh['coil'=32,'slab'=8] {'coil','slab'}, use_global_device_ids=true, to_apply=%region_6.7 | all-reduce | flops 4 | bytes 32 | tf_op jit(solution)/shard_map/psum | solution.py:119
  595.3 2.1 fusion.12
  597.4 140.0 %psum.55 = f32[2,32,32]{2,1,0:T(8,128)S(1)} all-reduce(f32[2,32,32]{2,1,0:T(8,128)S(1)} %pad_maximum_fusion.7), channel_id=1, replica_groups=mesh['coil'=32,'slab'=8] {'coil'}, use_global_device_ids=true, to_apply=%region_17.18 | all-reduce | flops 2048 | bytes 16384 | tf_op jit(solution)/shard_map/psum | solution.py:128
  741.3 2.3 fusion.14
  744.7 2.0 fusion.64
  (57 shorter events, 20.2 us)
Async XLA Ops:
  7.2 83.4 %all-gather.4.cloned.1.call-start = ((), (), s32[]{:S(2)}) async-start(), calls=%async_computation.4 | async-start | bytes 1081344 | tf_op jit(solution)/shard_map/all_gather | solution.py:74
  9.4 169.6 %all-gather.8.cloned.1.call-start = ((), (), s32[]{:S(2)}) async-start(), calls=%async_computation.6 | async-start | bytes 1081344 | tf_op jit(solution)/shard_map/all_gather | solution.py:74
  16.2 77.7 %copy-start.3 = (bf16[1,256,2,256]{3,1,0,2:T(8,128)(2,1)}, bf16[1,256,2,256]{3,1,0,2:T(8,128)(2,1)S(1)}, u32[]{:S(2)}) copy-start(bf16[1,256,2,256]{3,1,0,2:T(8,128)(2,1)S(1)} %get-tuple-element.47) | copy-start | bytes 786436
  112.1 6.5 copy-start.8
  112.2 6.6 copy-start.7
  112.2 20.0 %all-to-all-start = ((bf16[8,2,32768]{2,1,0:T(2,128)(2,1)}), bf16[8,2,32768]{2,1,0:T(2,128)(2,1)}, u32[]{:S(2)}, u32[]{:S(2)}) async-start(bf16[8,2,32768]{2,1,0:T(2,128)(2,1)} %reshape.272), calls=%async_computation | async-start | bytes 2097152 | tf_op jit(solution)/shard_map/all_to_all | solution.py:80
  152.0 4.4 copy-start.6
  173.2 20.2 %all-to-all-start.1 = ((bf16[8,2,32768]{2,1,0:T(2,128)(2,1)}), bf16[8,2,32768]{2,1,0:T(2,128)(2,1)}, u32[]{:S(2)}, u32[]{:S(2)}) async-start(bf16[8,2,32768]{2,1,0:T(2,128)(2,1)} %reshape.274), calls=%async_computation.1 | async-start | bytes 2097152 | tf_op jit(solution)/shard_map/all_to_all | solution.py:95
  178.7 189.4 %all-reduce.5.cloned.1.call-start = ((), (), s32[]{:S(2)}) async-start(), calls=%async_computation.7 | async-start | bytes 2097152
  213.4 2.2 copy-start.5
  215.6 1.6 copy-start.1
  219.2 1.7 copy-start.9
  219.2 148.9 %copy-start.4 = (f32[1,2,32,256]{3,2,1,0:T(8,128)S(1)}, f32[1,2,32,256]{3,2,1,0:T(8,128)}, u32[]{:S(2)}) copy-start(f32[1,2,32,256]{3,2,1,0:T(8,128)} %param.6) | copy-start | bytes 196612
  220.8 224.0 %all-gather.6.cloned.1.call-start = ((), (), s32[]{:S(2)}) async-start(), calls=%async_computation.5 | async-start | bytes 1081344 | tf_op jit(solution)/shard_map/all_gather | solution.py:74
  389.2 75.6 %all-to-all-start.3 = ((bf16[8,2,32768]{2,1,0:T(2,128)(2,1)}), bf16[8,2,32768]{2,1,0:T(2,128)(2,1)}, u32[]{:S(2)}, u32[]{:S(2)}) async-start(bf16[8,2,32768]{2,1,0:T(2,128)(2,1)} %reshape.278), calls=%async_computation.3 | async-start | bytes 2097152 | tf_op jit(solution)/shard_map/all_to_all | solution.py:80
  464.8 27.3 %all-to-all-start.2 = ((bf16[8,2,32768]{2,1,0:T(2,128)(2,1)}), bf16[8,2,32768]{2,1,0:T(2,128)(2,1)}, u32[]{:S(2)}, u32[]{:S(2)}) async-start(bf16[8,2,32768]{2,1,0:T(2,128)(2,1)} %reshape.276), calls=%async_computation.2 | async-start | bytes 2097152 | tf_op jit(solution)/shard_map/all_to_all | solution.py:80
  483.3 5.4 copy-start.2
  505.8 6.3 copy-start
Sparse Core Ops, SparseCore 0:
  11.1 79.3 all-gather.3
  93.1 73.8 all-gather.7
  221.0 147.1 all-reduce.4
  371.2 73.5 all-gather.5
where the time goes:
time: 763 us; the launch traced here: 753 us
  blocking collectives  288 us (38%)
  waiting for transfers between devices  219 us (29%)
  local copies, waits for them, and re-layouts  143 us (19%)
  other arithmetic  33.3 us (4%)
  matrix products  27.2 us (4%)
  between operations  21.9 us (3%)
  starting transfers between devices  21.2 us (3%)
    psum x1, blocking collectives, shards(): lax.psum(jnp.stack([line_terms(first_k), line_terms(second_k)]), 'coil')  140 us
    all_gather x3, waiting for transfers between devices, gathered_front(): return front(lax.all_gather(shard, 'coil', axis=0, tiled=True))  125 us
    psum x1, blocking collectives, shards(): lax.psum((jnp.sum(residual * residual), jnp.sum(residual * direction), jn...  74.5 us
    psum x1, blocking collectives, shards(): lax.psum((jnp.sum(direction * direction), jnp.sum(first_w * first_w)), both)  73.8 us
    unnamed x5, waiting for transfers between devices  71.1 us
    unnamed x30, local copies, waits for them, and re-layouts  61.8 us
    all_to_all x6, local copies, waits for them, and re-layouts, to_kspace(): lax.all_to_all(mixed, 'slab', split_axis=3, concat_axis=2, tiled=True)  38 us
    convert_element_type x3, local copies, waits for them, and re-layouts, to_kspace(): mixed = jnp.einsum('nixk,inom->moxk', rows, z_fwd, preferred_element_type...  21 us
  transfers between devices with their start and end apart: 8, of which 5 were waited for; matrix products, arithmetic and copies ran while one was open for 18% of the time, Pallas kernels for 0%

commit v1 on v0

--- a/solution.py
+++ b/solution.py
@@ -71,7 +71,11 @@
         ).astype(jnp.bfloat16)
 
     def gathered_front(shard):
-        return front(lax.all_gather(shard, "coil", axis=0, tiled=True))
+        return front(
+            jnp.concatenate(
+                lax.all_to_all(jnp.stack([shard] * lax.axis_size("coil")), "coil", 0, 0), axis=0
+            )
+        )
 
     def to_kspace(rows):
         mixed = jnp.einsum(

time: 763 us -> 698 us (0.915)
  waiting for transfers between devices: 219 us -> 125 us
  starting transfers between devices: 21.2 us -> 44.6 us
    all_gather x3 -> x0, waiting for transfers between devices: 125 us -> none  [gathered_front(): return front(lax.all_gather(shard, 'coil', axis=0, tiled=True))]
    all_to_all x0 -> x3, waiting for transfers between devices: none -> 28.3 us  [gathered_front(): lax.all_to_all(jnp.stack([shard] * lax.axis_size('coil')), 'coil', 0, 0)]
    all_to_all x0 -> x3, starting transfers between devices: none -> 23.6 us  [gathered_front(): lax.all_to_all(jnp.stack([shard] * lax.axis_size('coil')), 'coil', 0, 0)]
    unnamed x5 -> x2, waiting for transfers between devices: 71.1 us -> 71.7 us
    unnamed x30 -> x40, local copies, waits for them, and re-layouts: 61.8 us -> 62 us
  transfers between devices with their start and end apart: 8 -> 8, of which waited for: 5 -> 5; matrix products, arithmetic and copies ran while one was open for 18% -> 17% of each run, Pallas kernels for 0% -> 0%
where the time goes in v1:
time: 698 us; the launch traced here: 688 us
  blocking collectives  293 us (42%)
  local copies, waits for them, and re-layouts  146 us (21%)
  waiting for transfers between devices  125 us (18%)
  starting transfers between devices  44.6 us (6%)
  other arithmetic  30.1 us (4%)
  matrix products  27.1 us (4%)
  between operations  22.2 us (3%)
    psum x1, blocking collectives, shards(): lax.psum(jnp.stack([line_terms(first_k), line_terms(second_k)]), 'coil')  142 us
    psum x1, blocking collectives, shards(): lax.psum((jnp.sum(direction * direction), jnp.sum(first_w * first_w)), both)  76.9 us
    psum x1, blocking collectives, shards(): lax.psum((jnp.sum(residual * residual), jnp.sum(residual * direction), jn...  74.4 us
    unnamed x2, waiting for transfers between devices  71.7 us
    unnamed x40, local copies, waits for them, and re-layouts  62 us
    all_to_all x6, local copies, waits for them, and re-layouts, to_kspace(): lax.all_to_all(mixed, 'slab', split_axis=3, concat_axis=2, tiled=True)  37.8 us
    all_to_all x3, waiting for transfers between devices, gathered_front(): lax.all_to_all(jnp.stack([shard] * lax.axis_size('coil')), 'coil', 0, 0)  28.3 us
    all_to_all x3, starting transfers between devices, gathered_front(): lax.all_to_all(jnp.stack([shard] * lax.axis_size('coil')), 'coil', 0, 0)  23.6 us
  transfers between devices with their start and end apart: 8, of which 5 were waited for; matrix products, arithmetic and copies ran while one was open for 17% of the time, Pallas kernels for 0%

profile of v1, /device:TPU:2, one launch (start us, length us, event | category | flops | bytes accessed | tf_op | source)
XLA Modules:
  0.0 688.3 jit_solution(16948224562066434939)
XLA Ops:
  9.8 11.5 %all-to-all-start = ((bf16[32,1,2,32,256]{4,3,2,1,0:T(8,128)(2,1)}), bf16[32,1,2,32,256]{4,3,2,1,0:T(8,128)(2,1)S(1)}, u32[]{:S(2)}, u32[]{:S(2)}) async-start(bf16[32,1,2,32,256]{4,3,2,1,0:T(8,128)(2,1)} %stack.94), calls=%async_computation | async-start | bytes 2097152 | tf_op jit(solution)/shard_map/all_to_all | solution.py:76
  26.3 23.1 %all-to-all-done = bf16[32,1,2,32,256]{4,3,2,1,0:T(8,128)(2,1)S(1)} async-done(((bf16[32,1,2,32,256]{4,3,2,1,0:T(8,128)(2,1)}), bf16[32,1,2,32,256]{4,3,2,1,0:T(8,128)(2,1)S(1)}, u32[]{:S(2)}, u32[]{:S(2)}) %all-to-all-start) | async-done | bytes 1048608 | tf_op jit(solution)/shard_map/all_to_all | solution.py:76
  51.3 3.0 fusion.4
  54.3 7.2 %copy.46 = bf16[32,2,32,256]{0,2,1,3:T(8,128)(2,1)} copy(bf16[32,2,32,256]{3,0,2,1:T(8,128)(2,1)} %fusion.4) | data formatting | bytes 2097152 | tf_op jit(solution)/shard_map/convert_element_type | solution.py:83
  61.6 7.8 %reshape.293 = bf16[8,2,32768]{2,1,0:T(2,128)(2,1)} reshape(bf16[256,2,32,32]{3,2,1,0:T(8,128)(2,1)} %bitcast.309) | data formatting | bytes 2097152
  69.4 5.0 all-to-all-start.1
  74.4 14.5 %all-to-all-done.1 = bf16[8,2,32768]{2,1,0:T(2,128)(2,1)S(1)} async-done(((bf16[8,2,32768]{2,1,0:T(2,128)(2,1)}), bf16[8,2,32768]{2,1,0:T(2,128)(2,1)S(1)}, u32[]{:S(2)}, u32[]{:S(2)}) %all-to-all-start.1) | async-done | bytes 1048608 | tf_op jit(solution)/shard_map/all_to_all | solution.py:84
  90.1 6.1 all-to-all-start.5
  96.2 2.1 pad_maximum_fusion.2
  100.1 7.0 %reshape.294 = bf16[256,2,32,32]{3,2,1,0:T(8,128)(2,1)} reshape(bf16[8,2,32768]{2,1,0:T(2,128)(2,1)} %copy-done.3) | data formatting | bytes 2097152
  107.1 6.6 copy.47
  113.7 6.2 reshape.264
  119.9 4.4 fusion.2
  126.0 7.2 %copy.50 = bf16[32,2,256,32]{3,0,1,2:T(8,128)(2,1)} copy(bf16[32,2,256,32]{2,3,0,1:T(8,128)(2,1)} %fusion.9) | data formatting | bytes 2097152 | tf_op jit(solution)/shard_map/convert_element_type | solution.py:98
  133.3 7.8 %reshape.295 = bf16[8,2,32768]{2,1,0:T(2,128)(2,1)} reshape(bf16[256,2,32,32]{3,2,1,0:T(8,128)(2,1)} %bitcast.310) | data formatting | bytes 2097152
  141.1 5.6 all-to-all-start.2
  147.2 3.2 bitcast_convert_fusion.8
  150.4 10.9 %all-to-all-done.2 = bf16[8,2,32768]{2,1,0:T(2,128)(2,1)} async-done(((bf16[8,2,32768]{2,1,0:T(2,128)(2,1)}), bf16[8,2,32768]{2,1,0:T(2,128)(2,1)}, u32[]{:S(2)}, u32[]{:S(2)}) %all-to-all-start.2) | async-done | bytes 1048608 | tf_op jit(solution)/shard_map/all_to_all | solution.py:99
  161.3 7.0 %reshape.296 = bf16[256,2,32,32]{3,2,1,0:T(8,128)(2,1)} reshape(bf16[8,2,32768]{2,1,0:T(2,128)(2,1)} %all-to-all-done.2) | data formatting | bytes 2097152
  168.3 6.9 copy.124
  175.2 6.2 all_to_all.69
  181.4 2.2 fusion.5
  189.5 76.9 %all-reduce.2 = (f32[]{:T(128)}, f32[]{:T(128)}) all-reduce(f32[]{:T(128)} %get-tuple-element.46, f32[]{:T(128)} %get-tuple-element.37), channel_id=1, replica_groups=mesh['coil'=32,'slab'=8] {'coil','slab'}, use_global_device_ids=true, to_apply=%region_1.2 | all-reduce | flops 2 | bytes 16 | tf_op jit(solution)/shard_map/psum | solution.py:92
  268.3 71.7 %all-reduce.5.cloned.1.call-done = bf16[32,2,32,256]{3,2,0,1:T(8,128)(2,1)} async-done(((bf16[32,2,32,256]{3,2,0,1:T(8,128)(2,1)}), bf16[32,2,32,256]{3,2,0,1:T(8,128)(2,1)}) %all-reduce.5.cloned.1.call-update) | async-done | bytes 1048592
  340.0 2.2 fusion.61
  343.3 6.0 all-to-all-start.3
  349.3 3.3 fusion.7
  352.6 7.2 %copy.67 = bf16[32,2,32,256]{0,2,1,3:T(8,128)(2,1)} copy(bf16[32,2,32,256]{3,0,2,1:T(8,128)(2,1)} %fusion.7) | data formatting | bytes 2097152 | tf_op jit(solution)/shard_map/convert_element_type | solution.py:83
  359.8 7.8 %reshape.299 = bf16[8,2,32768]{2,1,0:T(2,128)(2,1)} reshape(bf16[256,2,32,32]{3,2,1,0:T(8,128)(2,1)} %bitcast.311) | data formatting | bytes 2097152
  367.6 5.2 all-to-all-done.3
  372.8 4.8 all-to-all-start.6
  381.0 2.3 fusion.6
  383.3 6.5 copy.61
  389.8 7.8 %reshape.297 = bf16[8,2,32768]{2,1,0:T(2,128)(2,1)} reshape(bf16[256,2,32,32]{3,2,1,0:T(8,128)(2,1)} %bitcast.312) | data formatting | bytes 2097152
  397.6 5.1 all-to-all-start.4
  402.7 7.0 %reshape.300 = bf16[256,2,32,32]{3,2,1,0:T(8,128)(2,1)} reshape(bf16[8,2,32768]{2,1,0:T(2,128)(2,1)} %all-to-all-done.6) | data formatting | bytes 2097152
  409.7 6.6 copy.68
  416.3 5.4 reshape.285
  421.8 3.4 fusion
  425.1 7.0 %reshape.298 = bf16[256,2,32,32]{3,2,1,0:T(8,128)(2,1)} reshape(bf16[8,2,32768]{2,1,0:T(2,128)(2,1)} %all-to-all-done.4) | data formatting | bytes 2097152
  432.2 6.6 copy.62
  438.8 6.3 reshape.279
  445.1 6.2 multiply_reduce_fusion
  451.3 74.4 %all-reduce.1 = (f32[]{:T(128)}, f32[]{:T(128)}, f32[]{:T(128)}, f32[]{:T(128)}) all-reduce(f32[]{:T(128)} %get-tuple-element.17, f32[]{:T(128)} %get-tuple-element.13, f32[]{:T(128)} %get-tuple-element.12, f32[]{:T(128)} %get-tuple-element.16), channel_id=1, replica_groups=mesh['coil'=32,'slab'=8] {'coil','slab'}, use_global_device_ids=true, to_apply=%region_6.7 | all-reduce | flops 4 | bytes 32 | tf_op jit(solution)/shard_map/psum | solution.py:123
  528.3 2.1 fusion.12
  530.4 141.6 %psum.55 = f32[2,32,32]{2,1,0:T(8,128)S(1)} all-reduce(f32[2,32,32]{2,1,0:T(8,128)S(1)} %pad_maximum_fusion.7), channel_id=1, replica_groups=mesh['coil'=32,'slab'=8] {'coil'}, use_global_device_ids=true, to_apply=%region_17.18 | all-reduce | flops 2048 | bytes 16384 | tf_op jit(solution)/shard_map/psum | solution.py:132
  675.8 2.3 fusion.14
  679.1 2.1 fusion.64
  (67 shorter events, 26.8 us)
Async XLA Ops:
  9.8 39.5 %all-to-all-start = ((bf16[32,1,2,32,256]{4,3,2,1,0:T(8,128)(2,1)}), bf16[32,1,2,32,256]{4,3,2,1,0:T(8,128)(2,1)S(1)}, u32[]{:S(2)}, u32[]{:S(2)}) async-start(bf16[32,1,2,32,256]{4,3,2,1,0:T(8,128)(2,1)} %stack.94), calls=%async_computation | async-start | bytes 2097152 | tf_op jit(solution)/shard_map/all_to_all | solution.py:76
  21.3 4.3 copy-start.5
  21.6 29.7 %copy-start.12 = (bf16[1,32,2,32]{1,3,0,2:T(8,128)(2,1)}, bf16[1,32,2,32]{1,3,0,2:T(8,128)(2,1)S(1)}, u32[]{:S(2)}) copy-start(bf16[1,32,2,32]{1,3,0,2:T(8,128)(2,1)S(1)} %get-tuple-element.55) | copy-start | bytes 12292
  50.0 1.4 copy-start.4
  69.4 5.0 copy-start.10
  69.4 19.4 %all-to-all-start.1 = ((bf16[8,2,32768]{2,1,0:T(2,128)(2,1)}), bf16[8,2,32768]{2,1,0:T(2,128)(2,1)S(1)}, u32[]{:S(2)}, u32[]{:S(2)}) async-start(bf16[8,2,32768]{2,1,0:T(2,128)(2,1)} %reshape.293), calls=%async_computation.1 | async-start | bytes 2097152 | tf_op jit(solution)/shard_map/all_to_all | solution.py:84
  88.9 9.4 %copy-start.3 = (bf16[8,2,32768]{2,1,0:T(2,128)(2,1)}, bf16[8,2,32768]{2,1,0:T(2,128)(2,1)S(1)}, u32[]{:S(2)}) copy-start(bf16[8,2,32768]{2,1,0:T(2,128)(2,1)S(1)} %all-to-all-done.1) | copy-start | bytes 3145732
  90.1 8.2 %copy-start.11 = (s32[32,32]{1,0:T(8,128)S(1)}, s32[32,32]{1,0:T(8,128)}, u32[]{:S(2)}) copy-start(s32[32,32]{1,0:T(8,128)} %param.11) | copy-start | bytes 12292
  90.1 8.3 %copy-start.9 = (f32[32,32]{1,0:T(8,128)S(1)}, f32[32,32]{1,0:T(8,128)}, u32[]{:S(2)}) copy-start(f32[32,32]{1,0:T(8,128)} %param.10) | copy-start | bytes 12292
  90.1 51.0 %all-to-all-start.5 = ((bf16[32,1,2,32,256]{4,3,2,1,0:T(8,128)(2,1)}), bf16[32,1,2,32,256]{4,3,2,1,0:T(8,128)(2,1)}, u32[]{:S(2)}, u32[]{:S(2)}) async-start(bf16[32,1,2,32,256]{4,3,2,1,0:T(8,128)(2,1)} %stack.109), calls=%async_computation.5 | async-start | bytes 2097152 | tf_op jit(solution)/shard_map/all_to_all | solution.py:76
  119.9 4.4 copy-start.8
  141.1 20.2 %all-to-all-start.2 = ((bf16[8,2,32768]{2,1,0:T(2,128)(2,1)}), bf16[8,2,32768]{2,1,0:T(2,128)(2,1)}, u32[]{:S(2)}, u32[]{:S(2)}) async-start(bf16[8,2,32768]{2,1,0:T(2,128)(2,1)} %reshape.295), calls=%async_computation.2 | async-start | bytes 2097152 | tf_op jit(solution)/shard_map/all_to_all | solution.py:99
  146.7 193.3 %all-reduce.5.cloned.1.call-start = ((), (), s32[]{:S(2)}) async-start(), calls=%async_computation.7 | async-start | bytes 2097152
  181.3 2.2 copy-start.7
  183.5 1.6 copy-start.1
  187.2 1.6 copy-start.14
  187.2 152.8 %copy-start.6 = (f32[1,2,32,256]{3,2,1,0:T(8,128)S(1)}, f32[1,2,32,256]{3,2,1,0:T(8,128)}, u32[]{:S(2)}) copy-start(f32[1,2,32,256]{3,2,1,0:T(8,128)} %param.6) | copy-start | bytes 196612
  188.8 160.5 %copy-start.13 = (bf16[1,32,2,32]{1,3,0,2:T(8,128)(2,1)S(1)}, bf16[1,32,2,32]{1,3,0,2:T(8,128)(2,1)}, u32[]{:S(2)}) copy-start(bf16[1,32,2,32]{1,3,0,2:T(8,128)(2,1)} %copy-done.12) | copy-start | bytes 12292
  343.3 29.5 %all-to-all-start.3 = ((bf16[32,1,2,32,256]{4,3,2,1,0:T(8,128)(2,1)}), bf16[32,1,2,32,256]{4,3,2,1,0:T(8,128)(2,1)}, u32[]{:S(2)}, u32[]{:S(2)}) async-start(bf16[32,1,2,32,256]{4,3,2,1,0:T(8,128)(2,1)} %stack.107), calls=%async_computation.3 | async-start | bytes 2097152 | tf_op jit(solution)/shard_map/all_to_all | solution.py:76
  372.8 24.8 %all-to-all-start.6 = ((bf16[8,2,32768]{2,1,0:T(2,128)(2,1)}), bf16[8,2,32768]{2,1,0:T(2,128)(2,1)}, u32[]{:S(2)}, u32[]{:S(2)}) async-start(bf16[8,2,32768]{2,1,0:T(2,128)(2,1)} %reshape.299), calls=%async_computation.6 | async-start | bytes 2097152 | tf_op jit(solution)/shard_map/all_to_all | solution.py:84
  397.6 27.6 %all-to-all-start.4 = ((bf16[8,2,32768]{2,1,0:T(2,128)(2,1)}), bf16[8,2,32768]{2,1,0:T(2,128)(2,1)}, u32[]{:S(2)}, u32[]{:S(2)}) async-start(bf16[8,2,32768]{2,1,0:T(2,128)(2,1)} %reshape.297), calls=%async_computation.4 | async-start | bytes 2097152 | tf_op jit(solution)/shard_map/all_to_all | solution.py:84
  416.3 5.4 copy-start.2
  438.8 6.3 copy-start
Sparse Core Ops, SparseCore 0:
  188.9 151.0 all-reduce.4
